TPU v7x, 512 devices: a whole 4x8x8 slice. The times are simulated.
512 devices in a mesh: ctx: 64 (over x, z, core), kvh: 8 (over y).
Axes of the slice: x: 4, y: 8, z: 8, core: 2. Of those that a mesh axis runs over, the one named last changes fastest.
Arguments:
- queries: bfloat16 [32768, 8192], P('ctx', 'kvh')
- key_vector_rows: bfloat16 [32768, 1024], P('ctx', 'kvh')
- value_vector_rows: bfloat16 [32768, 1024], P('ctx', 'kvh'), may hold values from -6 to 6
- block_picks: int32 [256, 8], P('ctx'), may hold values from 0 to 255, as said below
Outputs:
- attended: bfloat16 [32768, 8192], P(('ctx', 'kvh'))
Inputs may be any that keep to these rules, and one draw needn't show every extreme that they name: block_picks[b, 0] = b. The other entries of a row name 7 distinct blocks that lie on other indices of ctx (block c lies on index c // 4). Over the 4 rows of one index of ctx, the entries naming blocks of any one other index are at most 2 and name at most 1 distinct blocks; both bounds are reached in every draw.
All inputs are finite; a program needn't handle non-finite values.
Results may differ from a plain program's by a relative error of at most 0.0047.
Values may be sent and summed in bfloat16 or wider, within the bound.
No kernel may reach another device: no remote copies, remote signals or barrier semaphores. Data moves between devices by JAX's collectives and lax.ppermute only.
A program may use at most 64 MiB of HBM per device.

v0:
```python
import math
import jax
import jax.numpy as jnp
from jax import lax
from jax.sharding import PartitionSpec as P

HEAD_SIZE = 128
BLOCK_TOKENS = 128
PICKED_BLOCKS = 8


def plan_each(remote, blocks, peer_count, capacity):
    flat_picks = remote.reshape(-1)
    owners = flat_picks // blocks
    local_ids = flat_picks % blocks
    owner_hits = (owners[:, None] == jnp.arange(peer_count, dtype=jnp.int32)[None, :]).astype(
        jnp.int32
    )
    running = jnp.cumsum(owner_hits, axis=0) * owner_hits
    slot_rank = jnp.sum(running, axis=1) - 1
    slot_hits = (slot_rank[:, None] == jnp.arange(capacity, dtype=jnp.int32)[None, :]).astype(
        jnp.int32
    )
    requests = jnp.dot((owner_hits * local_ids[:, None]).T, slot_hits)
    return (requests, slot_rank)


def block_attention(query_block, kv_block, kv_heads):
    block_len = query_block.shape[0]
    pick_count = kv_block.shape[0]
    group_size = query_block.shape[1] // (kv_heads * HEAD_SIZE)
    query_heads = query_block.reshape(block_len, kv_heads, group_size, HEAD_SIZE)
    stacked = kv_block.reshape(pick_count * block_len, 2, kv_heads, HEAD_SIZE)
    key_selection = stacked[:, 0]
    value_selection = stacked[:, 1]
    scores = jnp.einsum(
        "qgxd,kgd->gxqk", query_heads, key_selection, preferred_element_type=jnp.float32
    )
    scores = scores * (1.0 / math.sqrt(HEAD_SIZE))
    positions = jnp.arange(block_len, dtype=jnp.int32)
    causal = positions[None, :] <= positions[:, None]
    visible = jnp.concatenate(
        [causal, jnp.ones((block_len, (pick_count - 1) * block_len), dtype=bool)], axis=1
    )
    scores = jnp.where(visible, scores, -jnp.inf)
    row_max = jnp.max(scores, axis=-1, keepdims=True)
    exponents = jnp.exp(scores - row_max)
    totals = jnp.sum(exponents, axis=-1, keepdims=True)
    weights = exponents.astype(jnp.bfloat16)
    blended = jnp.einsum(
        "gxqk,kgd->qgxd", weights, value_selection, preferred_element_type=jnp.float32
    )
    blended = blended / jnp.transpose(totals, (2, 0, 1, 3))
    return blended.reshape(block_len, -1).astype(jnp.bfloat16)


def body(queries, key_vector_rows, value_vector_rows, block_picks):
    peer_count = lax.axis_size("ctx")
    my_index = lax.axis_index("ctx")
    tok_dev = key_vector_rows.shape[0]
    blocks = tok_dev // BLOCK_TOKENS
    kv_heads = key_vector_rows.shape[1] // HEAD_SIZE
    local_kv = jnp.concatenate([key_vector_rows, value_vector_rows], axis=1).reshape(
        blocks, BLOCK_TOKENS, 2 * kv_heads * HEAD_SIZE
    )
    remote = block_picks[:, 1:]
    far_count = blocks * (PICKED_BLOCKS - 1)
    distinct_cap = (far_count // 2 + peer_count - 2) // (peer_count - 1)
    capacity = 2 * distinct_cap
    requests, slot_rank = plan_each(remote, blocks, peer_count, capacity)
    pick_table = lax.all_gather(block_picks, "ctx", axis=0, tiled=True)
    all_rows = pick_table[:, 1:].reshape(peer_count, blocks, PICKED_BLOCKS - 1)

    def requests_of(rows_one):
        return plan_each(rows_one, blocks, peer_count, capacity)[0]

    all_requests = jax.vmap(requests_of)(all_rows)
    wanted = jnp.take(all_requests, my_index, axis=1)
    outgoing = local_kv[wanted]
    incoming = lax.all_to_all(outgoing, "ctx", split_axis=0, concat_axis=0, tiled=True)
    owners = (remote // blocks).reshape(-1)
    fetched = incoming.reshape(peer_count * capacity, BLOCK_TOKENS, -1)[
        owners * capacity + slot_rank
    ]
    fetched = fetched.reshape(blocks, PICKED_BLOCKS - 1, BLOCK_TOKENS, -1)
    chosen = jnp.concatenate([local_kv[:, None], fetched], axis=1)

    def attend_pair(pair):
        return block_attention(pair[0], pair[1], kv_heads)

    attended = lax.map(attend_pair, (queries.reshape(blocks, BLOCK_TOKENS, -1), chosen))
    attended = attended.reshape(tok_dev, -1)
    return lax.all_to_all(attended, "kvh", split_axis=0, concat_axis=1, tiled=True)


def solution(mesh):
    return jax.shard_map(
        body,
        mesh=mesh,
        in_specs=(P("ctx", "kvh"), P("ctx", "kvh"), P("ctx", "kvh"), P("ctx", None)),
        out_specs=P(("ctx", "kvh"), None),
        check_vma=False,
    )
```

profile of v0, /device:TPU:1, one launch (start us, length us, event | category | flops | bytes accessed | tf_op | source)
XLA Modules:
  0.0 326.1 jit_solution(9920349787377583914)
XLA Ops:
  0.0 57.4 %all-gather = s32[64,4,8]{2,1,0:T(4,128)S(1)} all-gather(s32[1,4,8]{2,1,0:T(4,128)} %bitcast.120), channel_id=1, replica_groups=mesh['ctx'=64,'kvh'=8] {'ctx'}, dimensions={0}, use_global_device_ids=true | all-gather | bytes 8320 | tf_op jit(solution)/shard_map/all_gather | solution.py:71
  57.7 1.3 select_reduce_fusion
  59.1 2.6 fusion.19
  62.2 6.3 %gather_fusion = bf16[128,128,256]{2,1,0:T(8,128)(2,1)} fusion(bf16[4,128,256]{2,1,0:T(8,128)(2,1)S(1)} %bitcast.108, s32[1024]{0:T(1024)S(1)} %pad_clamp_fusion.1), kind=kCustom, calls=%fused_computation | custom fusion | bytes 16777728 | tf_op jit(solution)/shard_map/gather | solution.py:79
  68.5 5.9 %all-to-all-start = ((bf16[64,2,128,256]{3,2,1,0:T(8,128)(2,1)}), bf16[64,2,128,256]{3,2,1,0:T(8,128)(2,1)}, u32[]{:S(2)}, u32[]{:S(2)}) async-start(bf16[64,2,128,256]{3,2,1,0:T(8,128)(2,1)} %bitcast.110), calls=%async_computation | async-start | bytes 16777216 | tf_op jit(solution)/shard_map/all_to_all | solution.py:80
  75.0 185.1 %all-to-all-done = bf16[64,2,128,256]{3,2,1,0:T(8,128)(2,1)} async-done(((bf16[64,2,128,256]{3,2,1,0:T(8,128)(2,1)}), bf16[64,2,128,256]{3,2,1,0:T(8,128)(2,1)}, u32[]{:S(2)}, u32[]{:S(2)}) %all-to-all-start) | async-done | bytes 8388640 | tf_op jit(solution)/shard_map/all_to_all | solution.py:80
  260.1 5.4 %gather_fusion.1 = bf16[28,128,256]{2,1,0:T(8,128)(2,1)} fusion(bf16[128,128,256]{2,1,0:T(8,128)(2,1)} %bitcast.22, s32[1024]{0:T(1024)S(1)} %pad_clamp_fusion), kind=kCustom, calls=%fused_computation.1 | custom fusion | bytes 3670128 | tf_op jit(solution)/shard_map/gather | solution.py:82
  265.5 1.7 pad_maximum_fusion
  267.2 21.8 %while.11 = (s32[]{:T(128)}, bf16[4,128,1024]{2,1,0:T(8,128)(2,1)}, bf16[4,8,128,256]{3,2,1,0:T(8,128)(2,1)S(1)}, bf16[4,128,1024]{2,1,0:T(8,128)(2,1)}, s32[]{:T(128)}, /*index=5*/pred[]{:T(512)}) while((s32[]{:T(128)}, bf16[4,128,1024]{2,1,0:T(8,128)(2,1)}, bf16[4,8,128,256]{3,2,1,0:T(8,128)(2,1)S(1)}, bf16[4,128,1024]{2,1,0:T(8,128)(2,1)}, ...), condition=%wide.region_7.8_spmd, body=%wide.region_4.7_spmd.sunk | while | flops 548681728 | bytes 19452492 | solution.py:91
  267.4 0.4 copy.68
  267.8 1.0 constant_dynamic-slice_fusion.4
  269.0 0.7 fusion.44
  269.8 0.9 fusion.45
  270.6 1.1 fusion.46
  271.9 0.7 constant_dynamic-update-slice_fusion.4
  273.2 1.0 constant_dynamic-slice_fusion.4
  274.4 0.7 fusion.44
  275.2 0.9 fusion.45
  276.1 1.1 fusion.46
  277.3 0.7 constant_dynamic-update-slice_fusion.4
  278.7 1.0 constant_dynamic-slice_fusion.4
  279.9 0.7 fusion.44
  280.6 0.9 fusion.45
  281.5 1.1 fusion.46
  282.8 0.7 constant_dynamic-update-slice_fusion.4
  284.1 1.0 constant_dynamic-slice_fusion.4
  285.3 0.7 fusion.44
  286.1 0.9 fusion.45
  286.9 1.1 fusion.46
  288.2 0.7 constant_dynamic-update-slice_fusion.4
  289.0 36.1 %all_to_all.24 = bf16[8,64,1024]{2,1,0:T(8,128)(2,1)S(1)} all-to-all(bf16[8,64,1024]{2,1,0:T(8,128)(2,1)} %bitcast.117), channel_id=1, replica_groups=mesh['ctx'=64,'kvh'=8] {'kvh'}, dimensions={0} | all-to-all | bytes 2097152 | tf_op jit(solution)/shard_map/all_to_all | solution.py:93
  325.0 1.1 copy.61
  (57 shorter events, 4.8 us)
Async XLA Ops:
  0.0 62.1 %copy-start = (bf16[512,128]{1,0:T(8,128)(2,1)S(1)}, bf16[512,128]{1,0:T(8,128)(2,1)}, u32[]{:S(2)}) copy-start(bf16[512,128]{1,0:T(8,128)(2,1)} %param.7) | copy-start | bytes 393220
  0.0 62.1 %copy-start.1 = (bf16[512,128]{1,0:T(8,128)(2,1)S(1)}, bf16[512,128]{1,0:T(8,128)(2,1)}, u32[]{:S(2)}) copy-start(bf16[512,128]{1,0:T(8,128)(2,1)} %param.8) | copy-start | bytes 393220
  68.5 5.9 %copy-start.2 = (s32[4,8]{1,0:T(4,128)S(1)}, s32[4,8]{1,0:T(4,128)}, u32[]{:S(2)}) copy-start(s32[4,8]{1,0:T(4,128)} %param.9) | copy-start | bytes 388
  68.5 191.6 %all-to-all-start = ((bf16[64,2,128,256]{3,2,1,0:T(8,128)(2,1)}), bf16[64,2,128,256]{3,2,1,0:T(8,128)(2,1)}, u32[]{:S(2)}, u32[]{:S(2)}) async-start(bf16[64,2,128,256]{3,2,1,0:T(8,128)(2,1)} %bitcast.110), calls=%async_computation | async-start | bytes 16777216 | tf_op jit(solution)/shard_map/all_to_all | solution.py:80
where the time goes:
time: 327 us; the launch traced here: 326 us
  waiting for transfers between devices  185 us (57%)
  blocking collectives  93.5 us (29%)
  local copies, waits for them, and re-layouts  24.2 us (7%)
  matrix products  10.1 us (3%)
  other arithmetic  6.97 us (2%)
  starting transfers between devices  5.87 us (2%)
    all_to_all x1, waiting for transfers between devices, body(): lax.all_to_all(outgoing, 'ctx', split_axis=0, concat_axis=0, tiled=True)  185 us
    all_gather x1, blocking collectives, body(): pick_table = lax.all_gather(block_picks, 'ctx', axis=0, tiled=True)  57.4 us
    all_to_all x1, blocking collectives, body(): lax.all_to_all(attended, 'kvh', split_axis=0, concat_axis=1, tiled=True)  36.1 us
  transfers between devices with their start and end apart: 1, of which 1 were waited for; matrix products, arithmetic and copies ran while one was open for 0% of the time, Pallas kernels for 0%

commit v1 on v0

--- a/solution.py
+++ b/solution.py
@@ -68,7 +68,9 @@
     distinct_cap = (far_count // 2 + peer_count - 2) // (peer_count - 1)
     capacity = 2 * distinct_cap
     requests, slot_rank = plan_each(remote, blocks, peer_count, capacity)
-    pick_table = lax.all_gather(block_picks, "ctx", axis=0, tiled=True)
+    pick_table = jnp.concatenate(
+        lax.all_to_all(jnp.stack([block_picks] * lax.axis_size("ctx")), "ctx", 0, 0), axis=0
+    )
     all_rows = pick_table[:, 1:].reshape(peer_count, blocks, PICKED_BLOCKS - 1)
 
     def requests_of(rows_one):

time: 327 us -> 295 us (0.902)
  blocking collectives: 93.5 us -> 36.1 us
  starting transfers between devices: 5.87 us -> 20.4 us
  waiting for transfers between devices: 185 us -> 194 us
    all_gather x1 -> x0, blocking collectives: 57.4 us -> none  [body(): pick_table = lax.all_gather(block_picks, 'ctx', axis=0, tiled=True)]
    all_to_all x0 -> x1, starting transfers between devices: none -> 14.8 us  [body(): lax.all_to_all(jnp.stack([block_picks] * lax.axis_size('ctx')), 'ctx', 0, 0)]
    all_to_all x0 -> x1, waiting for transfers between devices: none -> 8.45 us  [body(): lax.all_to_all(jnp.stack([block_picks] * lax.axis_size('ctx')), 'ctx', 0, 0)]
  transfers between devices with their start and end apart: 1 -> 2, of which waited for: 1 -> 2; matrix products, arithmetic and copies ran while one was open for 0% -> 1% of each run, Pallas kernels for 0% -> 0%
where the time goes in v1:
time: 295 us
  waiting for transfers between devices  194 us (66%)
  blocking collectives  36.1 us (12%)
  local copies, waits for them, and re-layouts  27.3 us (9%)
  starting transfers between devices  20.4 us (7%)
  matrix products  10.1 us (3%)
  other arithmetic  6.99 us (2%)
    all_to_all x1, waiting for transfers between devices, body(): lax.all_to_all(outgoing, 'ctx', split_axis=0, concat_axis=0, tiled=True)  185 us
    all_to_all x1, blocking collectives, body(): lax.all_to_all(attended, 'kvh', split_axis=0, concat_axis=1, tiled=True)  36.1 us
    all_to_all x1, starting transfers between devices, body(): lax.all_to_all(jnp.stack([block_picks] * lax.axis_size('ctx')), 'ctx', 0, 0)  14.8 us
    all_to_all x1, waiting for transfers between devices, body(): lax.all_to_all(jnp.stack([block_picks] * lax.axis_size('ctx')), 'ctx', 0, 0)  8.45 us
    gather x1, local copies, waits for them, and re-layouts, body(): outgoing = local_kv[wanted]  6.3 us
  transfers between devices with their start and end apart: 2, of which 2 were waited for; matrix products, arithmetic and copies ran while one was open for 1% of the time, Pallas kernels for 0%

profile of v1, /device:TPU:1, one launch (start us, length us, event | category | flops | bytes accessed | tf_op | source)
XLA Modules:
  0.0 294.9 jit_solution(17130398000729972316)
XLA Ops:
  0.0 1.4 stack.2
  1.4 14.8 %all-to-all-start = ((s32[64,4,8]{2,1,0:T(4,128)}), s32[64,4,8]{2,1,0:T(4,128)S(1)}, u32[]{:S(2)}, u32[]{:S(2)}) async-start(s32[64,4,8]{2,1,0:T(4,128)} %stack.2), calls=%async_computation | async-start | bytes 262144 | tf_op jit(solution)/shard_map/all_to_all | solution.py:72
  16.2 0.9 constant_dynamic-update-slice_fusion.2
  17.1 0.9 constant_dynamic-update-slice_fusion.1
  18.1 8.5 %all-to-all-done = s32[64,4,8]{2,1,0:T(4,128)S(1)} async-done(((s32[64,4,8]{2,1,0:T(4,128)}), s32[64,4,8]{2,1,0:T(4,128)S(1)}, u32[]{:S(2)}, u32[]{:S(2)}) %all-to-all-start) | async-done | bytes 8224 | tf_op jit(solution)/shard_map/all_to_all | solution.py:72
  26.8 1.3 select_reduce_fusion
  28.2 2.6 fusion.19
  31.2 6.3 %gather_fusion = bf16[128,128,256]{2,1,0:T(8,128)(2,1)} fusion(bf16[4,128,256]{2,1,0:T(8,128)(2,1)S(1)} %bitcast.107, s32[1024]{0:T(1024)S(1)} %pad_clamp_fusion.1), kind=kCustom, calls=%fused_computation | custom fusion | bytes 16777728 | tf_op jit(solution)/shard_map/gather | solution.py:81
  37.6 5.6 %all-to-all-start.1 = ((bf16[64,2,128,256]{3,2,1,0:T(8,128)(2,1)}), bf16[64,2,128,256]{3,2,1,0:T(8,128)(2,1)}, u32[]{:S(2)}, u32[]{:S(2)}) async-start(bf16[64,2,128,256]{3,2,1,0:T(8,128)(2,1)} %bitcast.109), calls=%async_computation.1 | async-start | bytes 16777216 | tf_op jit(solution)/shard_map/all_to_all | solution.py:82
  43.8 185.2 %all-to-all-done.1 = bf16[64,2,128,256]{3,2,1,0:T(8,128)(2,1)} async-done(((bf16[64,2,128,256]{3,2,1,0:T(8,128)(2,1)}), bf16[64,2,128,256]{3,2,1,0:T(8,128)(2,1)}, u32[]{:S(2)}, u32[]{:S(2)}) %all-to-all-start.1) | async-done | bytes 8388640 | tf_op jit(solution)/shard_map/all_to_all | solution.py:82
  229.0 5.4 %gather_fusion.1 = bf16[28,128,256]{2,1,0:T(8,128)(2,1)} fusion(bf16[128,128,256]{2,1,0:T(8,128)(2,1)} %bitcast.21, s32[1024]{0:T(1024)S(1)} %pad_clamp_fusion), kind=kCustom, calls=%fused_computation.1 | custom fusion | bytes 3670128 | tf_op jit(solution)/shard_map/gather | solution.py:84
  234.3 1.7 pad_maximum_fusion
  236.0 21.8 %while.11 = (s32[]{:T(128)}, bf16[4,128,1024]{2,1,0:T(8,128)(2,1)}, bf16[4,8,128,256]{3,2,1,0:T(8,128)(2,1)S(1)}, bf16[4,128,1024]{2,1,0:T(8,128)(2,1)}, s32[]{:T(128)}, /*index=5*/pred[]{:T(512)}) while((s32[]{:T(128)}, bf16[4,128,1024]{2,1,0:T(8,128)(2,1)}, bf16[4,8,128,256]{3,2,1,0:T(8,128)(2,1)S(1)}, bf16[4,128,1024]{2,1,0:T(8,128)(2,1)}, ...), condition=%wide.region_7.8_spmd, body=%wide.region_4.7_spmd.sunk | while | flops 548681728 | bytes 19452492 | solution.py:93
  236.6 1.0 constant_dynamic-slice_fusion.4
  237.9 0.7 fusion.44
  238.6 0.9 fusion.45
  239.5 1.1 fusion.46
  240.8 0.7 constant_dynamic-update-slice_fusion.4
  242.1 1.0 constant_dynamic-slice_fusion.4
  243.3 0.7 fusion.44
  244.1 0.9 fusion.45
  244.9 1.1 fusion.46
  247.5 1.0 constant_dynamic-slice_fusion.4
  248.7 0.7 fusion.44
  249.5 0.9 fusion.45
  250.4 1.1 fusion.46
  253.0 1.0 constant_dynamic-slice_fusion.4
  254.2 0.7 fusion.44
  254.9 0.9 fusion.45
  255.8 1.1 fusion.46
  257.8 36.1 %all_to_all.29 = bf16[8,64,1024]{2,1,0:T(8,128)(2,1)S(1)} all-to-all(bf16[8,64,1024]{2,1,0:T(8,128)(2,1)} %bitcast.116), channel_id=1, replica_groups=mesh['ctx'=64,'kvh'=8] {'kvh'}, dimensions={0} | all-to-all | bytes 2097152 | tf_op jit(solution)/shard_map/all_to_all | solution.py:95
  293.9 1.1 copy.61
  (55 shorter events, 7.3 us)
Async XLA Ops:
  1.4 25.2 %all-to-all-start = ((s32[64,4,8]{2,1,0:T(4,128)}), s32[64,4,8]{2,1,0:T(4,128)S(1)}, u32[]{:S(2)}, u32[]{:S(2)}) async-start(s32[64,4,8]{2,1,0:T(4,128)} %stack.2), calls=%async_computation | async-start | bytes 262144 | tf_op jit(solution)/shard_map/all_to_all | solution.py:72
  37.6 5.6 %copy-start = (s32[4,8]{1,0:T(4,128)S(1)}, s32[4,8]{1,0:T(4,128)}, u32[]{:S(2)}) copy-start(s32[4,8]{1,0:T(4,128)} %param.9) | copy-start | bytes 388
  37.6 191.4 %all-to-all-start.1 = ((bf16[64,2,128,256]{3,2,1,0:T(8,128)(2,1)}), bf16[64,2,128,256]{3,2,1,0:T(8,128)(2,1)}, u32[]{:S(2)}, u32[]{:S(2)}) async-start(bf16[64,2,128,256]{3,2,1,0:T(8,128)(2,1)} %bitcast.109), calls=%async_computation.1 | async-start | bytes 16777216 | tf_op jit(solution)/shard_map/all_to_all | solution.py:82
